TPU v7x, 512 devices: a whole 4x4x16 slice. The times are simulated.
512 devices in a mesh: tm: 32 (over z, core), row: 16 (over x, y).
Axes of the slice: x: 4, y: 4, z: 16, core: 2. Of those that a mesh axis runs over, the one named last changes fastest.
Arguments:
- video: bfloat16 [32, 4, 384, 1024], P('tm', None, 'row'), may hold values from -6 to 6
- stem_weight: bfloat16 [64, 4, 3, 3], replicated, may hold values from -1 to 1
- w_qkv: bfloat16 [1536, 2304], P('tm'), may hold values from -0.15625 to 0.15625
- decay: float32 [32, 6], P('tm'), may hold values from 0.04 to 1, as said below
Outputs:
- mixed: bfloat16 [32, 32, 128, 768], P('tm', 'row')
Inputs may be any that keep to these rules, and one draw needn't show every extreme that they name: decay lies in (0, 1].
All inputs are finite; a program needn't handle non-finite values.
Results may differ from a plain program's by a relative error of at most 0.012.
Values may be sent and summed in bfloat16 or wider, within the bound.
A program may use at most 128 MiB of HBM per device.

v0:
```python
import jax
import jax.numpy as jnp
from jax import lax
from jax.sharding import PartitionSpec as P

HEADS = 6


def shifted(block, axis, distance):
    devices = range(lax.axis_size(axis))
    route = [(i - distance, i) for i in devices if i - distance in devices]
    return lax.ppermute(block, axis, route)


def prefix_2(x, axis, join, neutral):
    place = lax.axis_index(axis)
    gathered = jax.tree.map(
        lambda a, kind: lax.all_gather(a.astype(kind), axis), x, (jnp.bfloat16, jnp.bfloat16)
    )
    state = jax.tree.map(lambda a, e: jnp.zeros_like(a) + jnp.asarray(e, a.dtype), x, neutral)

    def one(step, state):
        return join(
            state,
            jax.tree.map(
                lambda a, own: lax.dynamic_index_in_dim(a, step, 0, False).astype(own.dtype),
                gathered,
                x,
            ),
        )

    return lax.fori_loop(0, place, one, state)


def combine(first_pair, later_pair):
    return (first_pair[0] * later_pair[0], later_pair[0] * first_pair[1] + later_pair[1])


def summarize(frame_rates, outer_sums):
    factor = jnp.ones_like(frame_rates[0])
    summed = jnp.zeros_like(outer_sums[0])
    factor = factor * frame_rates[0]
    summed = frame_rates[0] * summed + outer_sums[0]
    return (factor, summed)


def unroll(prefix, frame_rates, outer_sums):
    running = prefix
    running = frame_rates[0] * running + outer_sums[0]
    collected = [running]
    return jnp.stack(collected, axis=0)


def local(video, stem_weight, w_qkv, decay):
    frames_dev = video.shape[0]
    upper_row = shifted(video[:, :, -1:, :], "row", 1)
    padded = jnp.concatenate([upper_row, video], axis=2)
    padded = jnp.pad(padded, ((0, 0), (0, 0), (0, 0), (1, 0)))
    stem_out = lax.conv_general_dilated(
        padded,
        stem_weight,
        (2, 2),
        "VALID",
        dimension_numbers=("NCHW", "OIHW", "NCHW"),
        preferred_element_type=jnp.float32,
    )
    features = jnp.tanh(stem_out).astype(jnp.bfloat16)
    channels = features.shape[1]
    patch_rows = features.shape[2] // 6
    patch_cols = features.shape[3] // 4
    frame_tokens = patch_rows * patch_cols
    shaped = features.reshape(frames_dev, channels, patch_rows, 6, patch_cols, 4).transpose(
        0, 2, 4, 1, 3, 5
    )
    tokens = shaped.reshape(frames_dev * frame_tokens, channels * 24)
    qkv_width = w_qkv.shape[1]
    empty = jnp.zeros((tokens.shape[0], qkv_width), jnp.float32)
    block_rows = lax.all_gather(w_qkv, "tm", axis=0, tiled=True)
    columns = lax.slice_in_dim(tokens, 0, block_rows.shape[0], axis=1)
    projected = (empty + jnp.dot(columns, block_rows, preferred_element_type=jnp.float32)).astype(
        jnp.bfloat16
    )
    inner_width = qkv_width // 3
    head_size = inner_width // HEADS
    queries = projected[:, :inner_width].reshape(frames_dev, frame_tokens, HEADS, head_size)
    keys = projected[:, inner_width : 2 * inner_width].reshape(
        frames_dev, frame_tokens, HEADS, head_size
    )
    values = projected[:, 2 * inner_width :].reshape(frames_dev, frame_tokens, HEADS, head_size)
    kv_local = jnp.einsum("fnhd,fnhe->fhde", keys, values, preferred_element_type=jnp.float32)
    head_rates = decay[:, :, None, None]
    kv_total = lax.psum(kv_local.astype(jnp.bfloat16), "row").astype(jnp.float32)
    factor, summed = summarize(head_rates, kv_total)
    prefix = prefix_2(
        (factor, summed), "tm", combine, (jnp.ones_like(factor), jnp.zeros_like(summed))
    )[1]
    states = unroll(prefix, head_rates, kv_total).astype(jnp.bfloat16)
    attended = jnp.einsum("fnhd,fhde->fnhe", queries, states, preferred_element_type=jnp.float32)
    attended = attended * lax.rsqrt(jnp.mean(attended * attended, axis=-1, keepdims=True) + 1e-06)
    return attended.reshape(frames_dev, patch_rows, patch_cols, inner_width).astype(jnp.bfloat16)


def solution(mesh):
    return jax.shard_map(
        local,
        mesh=mesh,
        in_specs=(P("tm", None, "row", None), P(), P("tm", None), P("tm", None)),
        out_specs=P("tm", "row", None, None),
        check_vma=False,
    )
```

profile of v0, /device:TPU:491, one launch (start us, length us, event | category | flops | bytes accessed | tf_op | source)
XLA Modules:
  0.0 324.3 jit_solution(5156422705934072437)
XLA Ops:
  8.2 3.2 collective-permute-start
  11.4 1.3 collective-permute-done
  13.8 1.3 reshape.102
  15.1 4.3 %copy.74 = bf16[4,25,1,8,130]{3,0,4,1,2:T(4,128)(2,1)S(1)} copy(bf16[4,25,1,8,130]{4,3,1,0,2:T(8,128)(2,1)} %reshape.102) | data formatting | bytes 416000 | tf_op jit(solution)/shard_map/conv_general_dilated | solution.py:59
  19.6 5.0 %fusion.3 = f32[12,8,65,64]{3,1,2,0:T(8,128)} fusion(bf16[64,4,3,3]{0,1,3,2:T(4,128)(2,1)S(1)} %copy-done, bf16[4,25,1,7,2]{3,0,4,1,2:T(4,128)(2,1)S(1)} %slice.18, bf16[4,25,1,8,130]{3,0,4,1,2:T(4,128)(2,1)S(1)} %copy.74), kind=kOutput, calls=%fused_computation.7 | convolution fusion | flops 29387520 | bytes 1812848 | tf_op jit(solution)/shard_map/conv_general_dilated | solution.py:59
  24.5 3.4 %copy.75 = f32[12,8,65,64]{2,3,1,0:T(8,128)S(1)} copy(f32[12,8,65,64]{3,1,2,0:T(8,128)} %fusion.3) | data formatting | bytes 3194880 | tf_op jit(solution)/shard_map/conv_general_dilated | solution.py:59
  28.4 1.2 copy.76
  29.6 1.2 reshape.91
  31.8 1.3 copy.78
  33.0 52.2 %all-gather.5.cloned.1.call-done = bf16[1536,2304]{1,0:T(8,128)(2,1)} async-done(((bf16[48,2304]{1,0:T(8,128)(2,1)}), bf16[1536,2304]{1,0:T(8,128)(2,1)}) %all-gather.5.cloned.1.call-update) | async-done | bytes 7077904 | tf_op jit(solution)/shard_map/all_gather | solution.py:78
  85.2 5.0 %convolution_convert_fusion = bf16[256,2304]{1,0:T(8,128)(2,1)S(1)} fusion(bf16[1536,2304]{1,0:T(8,128)(2,1)} %all-gather.5.cloned.1.call-done, bf16[192,8,2,128]{3,2,1,0:T(2,128)(2,1)S(1)} %bitcast.66), kind=kOutput, calls=%fused_computation.4 | convolution fusion | flops 1812529152 | bytes 9043968 | tf_op jit(solution)/shard_map/dot_general | solution.py:80
  91.7 108.5 %all-reduce.2.cloned.1.call-done = bf16[1,6,128,128]{3,2,1,0:T(8,128)(2,1)} async-done(((bf16[1,6,128,128]{3,2,1,0:T(8,128)(2,1)}), bf16[1,6,128,128]{3,2,1,0:T(8,128)(2,1)}) %all-reduce.2.cloned.1.call-update) | async-done | bytes 196624 | tf_op jit(solution)/shard_map/psum | solution.py:92
  200.3 1.7 fusion.9
  202.0 30.6 %all-gather.1 = bf16[32,1,6]{2,1,0:T(2,128)(2,1)S(1)} all-gather(bf16[1,1,6]{2,1,0:T(2,128)(2,1)S(1)} %convert_bitcast_fusion.1), channel_id=2, replica_groups=mesh['tm'=32,'row'=16] {'tm'}, dimensions={0}, use_global_device_ids=true | all-gather | bytes 396 | tf_op jit(solution)/shard_map/all_gather | solution.py:18
  233.0 48.6 %all-gather.7.cloned.1.call-done = bf16[32,6,128,128]{3,2,1,0:T(8,128)(2,1)} async-done(((bf16[1,6,128,128]{3,2,1,0:T(8,128)(2,1)}), bf16[32,6,128,128]{3,2,1,0:T(8,128)(2,1)}) %all-gather.7.cloned.1.call-update) | async-done | bytes 6291472 | tf_op jit(solution)/shard_map/all_gather | solution.py:18
  281.7 34.4 %while.12 = (s32[]{:T(128)}, f32[6,128,128]{2,1,0:T(8,128)S(1)}, s32[]{:T(128)}, bf16[32,6,1,1]{1,3,2,0:T(2,128)(2,1)S(1)}, bf16[32,6,128,128]{3,2,1,0:T(8,128)(2,1)}, /*index=5*/s32[]{:T(128)}, s32[]{:T(128)}, s32[]{:T(128)}) while((s32[]{:T(128)}, f32[6,128,128]{2,1,0:T(8,128)S(1)}, s32[]{:T(128)}, bf16[32,6,1,1]{1,3,2,0:T(2,128)(2,1)S(1)}, ...), condition=%wide.region_2.3_spmd, body=%wide.region_1.2_spmd.sunk | while | flops 294923 | bytes 983227 | solution.py:32
  281.7 1.1 convert_add_fusion.3
  282.9 1.1 convert_add_fusion.3
  284.0 1.1 convert_add_fusion.3
  285.1 1.1 convert_add_fusion.3
  286.2 1.1 convert_add_fusion.3
  287.3 1.1 convert_add_fusion.3
  288.4 1.1 convert_add_fusion.3
  289.5 1.1 convert_add_fusion.3
  290.6 1.1 convert_add_fusion.3
  291.7 1.1 convert_add_fusion.3
  292.8 1.1 convert_add_fusion.3
  294.0 1.1 convert_add_fusion.3
  295.1 1.1 convert_add_fusion.3
  296.2 1.1 convert_add_fusion.3
  297.3 1.1 convert_add_fusion.3
  298.4 1.1 convert_add_fusion.3
  299.5 1.1 convert_add_fusion.3
  300.6 1.1 convert_add_fusion.3
  301.7 1.1 convert_add_fusion.3
  302.8 1.1 convert_add_fusion.3
  304.0 1.1 convert_add_fusion.3
  305.1 1.1 convert_add_fusion.3
  306.2 1.1 convert_add_fusion.3
  307.3 1.1 convert_add_fusion.3
  308.4 1.1 convert_add_fusion.3
  309.5 1.1 convert_add_fusion.3
  310.6 1.1 convert_add_fusion.3
  311.7 1.1 convert_add_fusion.3
  312.8 1.1 convert_add_fusion.3
  313.9 1.1 convert_add_fusion.3
  315.1 1.1 convert_add_fusion.3
  316.7 1.0 copy.86
  (66 shorter events, 6.9 us)
Async XLA Ops:
  6.5 13.0 %copy-start = (bf16[64,4,3,3]{0,1,3,2:T(4,128)(2,1)S(1)}, bf16[64,4,3,3]{0,1,3,2:T(4,128)(2,1)}, u32[]{:S(2)}) copy-start(bf16[64,4,3,3]{0,1,3,2:T(4,128)(2,1)} %param.7) | copy-start | bytes 13828
  6.5 78.7 %all-gather.5.cloned.1.call-start = ((), (), s32[]{:S(2)}) async-start(), calls=%async_computation | async-start | bytes 7299072 | tf_op jit(solution)/shard_map/all_gather | solution.py:78
  7.3 193.0 %all-reduce.2.cloned.1.call-start = ((), (), s32[]{:S(2)}) async-start(), calls=%async_computation.1 | async-start | bytes 393216 | tf_op jit(solution)/shard_map/psum | solution.py:92
  8.2 4.5 %collective-permute-start = (bf16[1,4,1,1024]{3,2,1,0:T(2,128)(2,1)S(1)}, bf16[1,4,1,1024]{3,2,1,0:T(2,128)(2,1)S(1)}, u32[]{:S(2)}, u32[]{:S(2)}) collective-permute-start(bf16[1,4,1,1024]{3,2,1,0:T(2,128)(2,1)S(1)} %slice.12), channel_id=1, source_target_pairs={{0,1},{1,2},{2,3},{3,4},{4,5},{5,6},{6,7},{7,8},{8,9},{9,10},{10,1... | collective-permute-start | bytes 24584 | tf_op jit(solution)/shard_map/ppermute | solution.py:12
  24.5 3.4 %copy-start.2 = (pred[8,65]{1,0:T(8,128)(4,1)S(1)}, pred[8,65]{1,0:T(8,128)(4,1)}, u32[]{:S(2)}) copy-start(pred[8,65]{1,0:T(8,128)(4,1)} %constant.40) | copy-start | bytes 1564
  90.3 1.5 copy-start.3
  91.7 190.0 %all-gather.7.cloned.1.call-start = ((), (), s32[]{:S(2)}) async-start(), calls=%async_computation.2 | async-start | bytes 6488064 | tf_op jit(solution)/shard_map/all_gather | solution.py:18
  202.0 114.2 %copy-start.1 = (bf16[1,6,128,128]{3,2,1,0:T(8,128)(2,1)S(1)}, bf16[1,6,128,128]{3,2,1,0:T(8,128)(2,1)}, u32[]{:S(2)}) copy-start(bf16[1,6,128,128]{3,2,1,0:T(8,128)(2,1)} %all-reduce.2.cloned.1.call-done) | copy-start | bytes 589828
Sparse Core Ops, SparseCore 0:
  9.5 75.6 all-gather.4
  91.8 108.4 all-reduce.1
  202.4 79.2 all-gather.6
where the time goes:
time: 326 us; the launch traced here: 324 us
  waiting for transfers between devices  211 us (65%)
  other arithmetic  36.6 us (11%)
  blocking collectives  30.6 us (9%)
  local copies, waits for them, and re-layouts  16.7 us (5%)
  between operations  13.3 us (4%)
  matrix products  11.4 us (3%)
  starting transfers between devices  3.29 us (1%)
    psum x1, waiting for transfers between devices, local(): lax.psum(kv_local.astype(jnp.bfloat16), 'row').astype(jnp.float32)  109 us
    all_gather x1, waiting for transfers between devices, local(): block_rows = lax.all_gather(w_qkv, 'tm', axis=0, tiled=True)  52.2 us
    all_gather x1, waiting for transfers between devices, prefix_2(): lax.all_gather(a.astype(kind), axis)  48.6 us
    add x31, other arithmetic, combine(): later_pair[0] * first_pair[1] + later_pair[1]  33.1 us
    all_gather x1, blocking collectives, prefix_2(): lax.all_gather(a.astype(kind), axis)  30.6 us
    conv_general_dilated x4, local copies, waits for them, and re-layouts, local(): lax.conv_general_dilated(padded, stem_weight, (2, 2), 'VALID', dimension_...  9.06 us
  transfers between devices with their start and end apart: 4, of which 4 were waited for; matrix products, arithmetic and copies ran while one was open for 7% of the time, Pallas kernels for 0%

commit v1 on v0

--- a/solution.py
+++ b/solution.py
@@ -89,7 +89,9 @@
     values = projected[:, 2 * inner_width :].reshape(frames_dev, frame_tokens, HEADS, head_size)
     kv_local = jnp.einsum("fnhd,fnhe->fhde", keys, values, preferred_element_type=jnp.float32)
     head_rates = decay[:, :, None, None]
-    kv_total = lax.psum(kv_local.astype(jnp.bfloat16), "row").astype(jnp.float32)
+    kv_total = jnp.sum(lax.all_gather(kv_local.astype(jnp.bfloat16), "row"), axis=0).astype(
+        jnp.float32
+    )
     factor, summed = summarize(head_rates, kv_total)
     prefix = prefix_2(
         (factor, summed), "tm", combine, (jnp.ones_like(factor), jnp.zeros_like(summed))

time: 326 us -> 275 us (0.84)
  the two profiles are of different devices: /device:TPU:491 before, /device:TPU:485 now
where the time goes in v1:
time: 275 us; the launch traced here: 274 us
  waiting for transfers between devices  162 us (59%)
  other arithmetic  38.2 us (14%)
  blocking collectives  28.6 us (10%)
  local copies, waits for them, and re-layouts  16.6 us (6%)
  between operations  13.3 us (5%)
  matrix products  11.4 us (4%)
  starting transfers between devices  3.29 us (1%)
    all_gather x1, waiting for transfers between devices, local(): lax.all_gather(kv_local.astype(jnp.bfloat16), 'row')  59.8 us
    all_gather x1, waiting for transfers between devices, local(): block_rows = lax.all_gather(w_qkv, 'tm', axis=0, tiled=True)  50.2 us
    all_gather x1, waiting for transfers between devices, prefix_2(): lax.all_gather(a.astype(kind), axis)  47.6 us
    add x31, other arithmetic, combine(): later_pair[0] * first_pair[1] + later_pair[1]  33.1 us
    all_gather x1, blocking collectives, prefix_2(): lax.all_gather(a.astype(kind), axis)  28.6 us
    conv_general_dilated x4, local copies, waits for them, and re-layouts, local(): lax.conv_general_dilated(padded, stem_weight, (2, 2), 'VALID', dimension_...  9.01 us
  transfers between devices with their start and end apart: 4, of which 4 were waited for; matrix products, arithmetic and copies ran while one was open for 8% of the time, Pallas kernels for 0%

profile of v1, /device:TPU:485, one launch (start us, length us, event | category | flops | bytes accessed | tf_op | source)
XLA Modules:
  0.0 274.1 jit_solution(16727308106365300755)
XLA Ops:
  8.2 3.2 %collective-permute-start = (bf16[1,4,1,1024]{3,2,1,0:T(2,128)(2,1)S(1)}, bf16[1,4,1,1024]{3,2,1,0:T(2,128)(2,1)S(1)}, u32[]{:S(2)}, u32[]{:S(2)}) collective-permute-start(bf16[1,4,1,1024]{3,2,1,0:T(2,128)(2,1)S(1)} %slice.12), channel_id=1, source_target_pairs={{0,1},{1,2},{2,3},{3,4},{4,5},{5,6},{6,7},{7,8},{8,9},{9,10},{10,1... | collective-permute-start | bytes 24584 | tf_op jit(solution)/shard_map/ppermute | solution.py:12
  11.4 3.4 %collective-permute-done = bf16[1,4,1,1024]{3,2,1,0:T(2,128)(2,1)S(1)} collective-permute-done((bf16[1,4,1,1024]{3,2,1,0:T(2,128)(2,1)S(1)}, bf16[1,4,1,1024]{3,2,1,0:T(2,128)(2,1)S(1)}, u32[]{:S(2)}, u32[]{:S(2)}) %collective-permute-start) | collective-permute-done | bytes 8224 | tf_op jit(solution)/shard_map/ppermute | solution.py:12
  15.9 1.3 reshape.125
  17.2 4.3 %copy.74 = bf16[4,25,1,8,130]{3,0,4,1,2:T(4,128)(2,1)S(1)} copy(bf16[4,25,1,8,130]{4,3,1,0,2:T(8,128)(2,1)} %reshape.125) | data formatting | bytes 416000 | tf_op jit(solution)/shard_map/conv_general_dilated | solution.py:59
  21.6 5.0 %fusion.3 = f32[12,8,65,64]{3,1,2,0:T(8,128)} fusion(bf16[64,4,3,3]{0,1,3,2:T(4,128)(2,1)S(1)} %copy-done, bf16[4,25,1,7,2]{3,0,4,1,2:T(4,128)(2,1)S(1)} %slice.18, bf16[4,25,1,8,130]{3,0,4,1,2:T(4,128)(2,1)S(1)} %copy.74), kind=kOutput, calls=%fused_computation.7 | convolution fusion | flops 29387520 | bytes 1812848 | tf_op jit(solution)/shard_map/conv_general_dilated | solution.py:59
  26.6 3.3 %copy.75 = f32[12,8,65,64]{2,3,1,0:T(8,128)S(1)} copy(f32[12,8,65,64]{3,1,2,0:T(8,128)} %fusion.3) | data formatting | bytes 3194880 | tf_op jit(solution)/shard_map/conv_general_dilated | solution.py:59
  30.4 1.2 copy.76
  31.7 1.2 reshape.111
  33.8 1.3 copy.78
  35.1 50.2 %all-gather.7.cloned.1.call-done = bf16[1536,2304]{1,0:T(8,128)(2,1)} async-done(((bf16[48,2304]{1,0:T(8,128)(2,1)}), bf16[1536,2304]{1,0:T(8,128)(2,1)}) %all-gather.7.cloned.1.call-update) | async-done | bytes 7077904 | tf_op jit(solution)/shard_map/all_gather | solution.py:78
  85.3 5.0 %convolution_convert_fusion = bf16[256,2304]{1,0:T(8,128)(2,1)S(1)} fusion(bf16[1536,2304]{1,0:T(8,128)(2,1)} %all-gather.7.cloned.1.call-done, bf16[192,8,2,128]{3,2,1,0:T(2,128)(2,1)S(1)} %bitcast.62), kind=kOutput, calls=%fused_computation.4 | convolution fusion | flops 1812529152 | bytes 9043968 | tf_op jit(solution)/shard_map/dot_general | solution.py:80
  91.8 59.8 %all-gather.11.cloned.1.call-done = bf16[96,128,128]{2,1,0:T(8,128)(2,1)} async-done(((bf16[6,128,128]{2,1,0:T(8,128)(2,1)}), bf16[96,128,128]{2,1,0:T(8,128)(2,1)}) %all-gather.11.cloned.1.call-update) | async-done | bytes 3145744 | tf_op jit(solution)/shard_map/all_gather | solution.py:92
  151.6 2.5 reduce.3
  154.9 28.6 %all-gather.2 = bf16[32,1,6]{2,1,0:T(2,128)(2,1)S(1)} all-gather(bf16[1,1,6]{2,1,0:T(2,128)(2,1)S(1)} %convert_bitcast_fusion.1), channel_id=2, replica_groups=mesh['tm'=32,'row'=16] {'tm'}, dimensions={0}, use_global_device_ids=true | all-gather | bytes 396 | tf_op jit(solution)/shard_map/all_gather | solution.py:18
  183.9 47.6 %all-gather.9.cloned.1.call-done = bf16[32,6,128,128]{3,2,1,0:T(8,128)(2,1)} async-done(((bf16[1,6,128,128]{3,2,1,0:T(8,128)(2,1)}), bf16[32,6,128,128]{3,2,1,0:T(8,128)(2,1)}) %all-gather.9.cloned.1.call-update) | async-done | bytes 6291472 | tf_op jit(solution)/shard_map/all_gather | solution.py:18
  231.5 34.4 %while.12 = (s32[]{:T(128)}, f32[6,128,128]{2,1,0:T(8,128)S(1)}, s32[]{:T(128)}, bf16[32,6,1,1]{1,3,2,0:T(2,128)(2,1)S(1)}, bf16[32,6,128,128]{3,2,1,0:T(8,128)(2,1)}, /*index=5*/s32[]{:T(128)}, s32[]{:T(128)}, s32[]{:T(128)}) while((s32[]{:T(128)}, f32[6,128,128]{2,1,0:T(8,128)S(1)}, s32[]{:T(128)}, bf16[32,6,1,1]{1,3,2,0:T(2,128)(2,1)S(1)}, ...), condition=%wide.region_2.3_spmd, body=%wide.region_1.2_spmd.sunk | while | flops 294923 | bytes 983227 | solution.py:32
  231.6 1.1 convert_add_fusion.3
  232.7 1.1 convert_add_fusion.3
  233.8 1.1 convert_add_fusion.3
  234.9 1.1 convert_add_fusion.3
  236.0 1.1 convert_add_fusion.3
  237.1 1.1 convert_add_fusion.3
  238.2 1.1 convert_add_fusion.3
  239.3 1.1 convert_add_fusion.3
  240.4 1.1 convert_add_fusion.3
  241.6 1.1 convert_add_fusion.3
  242.7 1.1 convert_add_fusion.3
  243.8 1.1 convert_add_fusion.3
  244.9 1.1 convert_add_fusion.3
  246.0 1.1 convert_add_fusion.3
  247.1 1.1 convert_add_fusion.3
  248.2 1.1 convert_add_fusion.3
  249.3 1.1 convert_add_fusion.3
  250.4 1.1 convert_add_fusion.3
  251.5 1.1 convert_add_fusion.3
  252.7 1.1 convert_add_fusion.3
  253.8 1.1 convert_add_fusion.3
  254.9 1.1 convert_add_fusion.3
  256.0 1.1 convert_add_fusion.3
  257.1 1.1 convert_add_fusion.3
  258.2 1.1 convert_add_fusion.3
  259.3 1.1 convert_add_fusion.3
  260.4 1.1 convert_add_fusion.3
  261.5 1.1 convert_add_fusion.3
  262.7 1.1 convert_add_fusion.3
  263.8 1.1 convert_add_fusion.3
  264.9 1.1 convert_add_fusion.3
  266.6 1.0 copy.86
  (65 shorter events, 7.7 us)
Async XLA Ops:
  6.5 15.1 %copy-start = (bf16[64,4,3,3]{0,1,3,2:T(4,128)(2,1)S(1)}, bf16[64,4,3,3]{0,1,3,2:T(4,128)(2,1)}, u32[]{:S(2)}) copy-start(bf16[64,4,3,3]{0,1,3,2:T(4,128)(2,1)} %param.7) | copy-start | bytes 13828
  6.5 78.7 %all-gather.7.cloned.1.call-start = ((), (), s32[]{:S(2)}) async-start(), calls=%async_computation | async-start | bytes 7299072 | tf_op jit(solution)/shard_map/all_gather | solution.py:78
  7.3 144.3 %all-gather.11.cloned.1.call-start = ((), (), s32[]{:S(2)}) async-start(), calls=%async_computation.2 | async-start | bytes 3342336 | tf_op jit(solution)/shard_map/all_gather | solution.py:92
  8.2 6.6 %collective-permute-start = (bf16[1,4,1,1024]{3,2,1,0:T(2,128)(2,1)S(1)}, bf16[1,4,1,1024]{3,2,1,0:T(2,128)(2,1)S(1)}, u32[]{:S(2)}, u32[]{:S(2)}) collective-permute-start(bf16[1,4,1,1024]{3,2,1,0:T(2,128)(2,1)S(1)} %slice.12), channel_id=1, source_target_pairs={{0,1},{1,2},{2,3},{3,4},{4,5},{5,6},{6,7},{7,8},{8,9},{9,10},{10,1... | collective-permute-start | bytes 24584 | tf_op jit(solution)/shard_map/ppermute | solution.py:12
  26.6 3.3 %copy-start.1 = (pred[8,65]{1,0:T(8,128)(4,1)S(1)}, pred[8,65]{1,0:T(8,128)(4,1)}, u32[]{:S(2)}) copy-start(pred[8,65]{1,0:T(8,128)(4,1)} %constant.42) | copy-start | bytes 1564
  90.3 1.5 copy-start.2
  91.7 139.7 %all-gather.9.cloned.1.call-start = ((), (), s32[]{:S(2)}) async-start(), calls=%async_computation.1 | async-start | bytes 6488064 | tf_op jit(solution)/shard_map/all_gather | solution.py:18
Sparse Core Ops, SparseCore 0:
  9.5 75.7 all-gather.6
  91.9 59.6 all-gather.10
  155.0 76.4 all-gather.8
